TPU v7x, 32 devices: a whole 2x2x4 slice. The times are simulated.
32 devices in a mesh: clip: 2 (over x), slab: 16 (over z, y, core).
Axes of the slice: x: 2, y: 2, z: 4, core: 2. Of those that a mesh axis runs over, the one named last changes fastest.
Arguments:
- mask_field: float32 [4096, 2048], P(('clip', 'slab')), parts along dimension 0, may hold values from -1.8 to 2.9
- target_print: int32 [4096, 2048], P(('clip', 'slab')), parts along dimension 0, may hold values from 0 to 1
- source_points: int32 [32, 2], P('clip'), parts along dimension 0, may hold values from 0 to 60
- source_groups: int32 [32], P('clip'), parts along dimension 0, may hold values from 0 to 7
- group_logits: float32 [16], P('clip'), parts along dimension 0, may hold values from -1 to 1
- pupil_radius: int32 [2], P('clip'), parts along dimension 0, may hold values from 32 to 127
Outputs:
- loss_value: float32 [2], P('clip'), parts along dimension 0
- mask_grad: float32 [4096, 2048], P(('clip', 'slab')), parts along dimension 0
- group_grad: float32 [16], P('clip'), parts along dimension 0
There are 2 independent parts, one for each index of `clip`. A program takes and returns all parts, laid end to end along the dimension named above; each array names one. Nothing has to cross between parts.
All inputs are finite; a program needn't handle non-finite values.
Results may differ from a plain program's by a relative error of at most 0.0003.
Values sent between devices are 32-bit elements; how exact they have to be, the bound alone decides.
A program may use at most 128 MiB of HBM per device.

v0:
```python
import math
import jax
import jax.numpy as jnp
from jax import lax
from jax.sharding import PartitionSpec as P

K = 256
GRID = 61
NG = 8
steepness = 8.0
threshold = 0.3
shift_scale = 45
full_turn = 2.0 * math.pi
highest = lax.Precision.HIGHEST


def contract(form, left, right):
    return jnp.einsum(form, left, right, precision=highest)


def turn_table(left, right, length):
    product = jnp.mod(left[:, None] * right[None, :], length)
    angles = full_turn * product.astype(jnp.float32) / length
    return (jnp.cos(angles), jnp.sin(angles))


def pupil_mask(shifted, radius_sq, along_first, along_second):
    first_axis = along_first[None, :, None] + shifted[:, 0, None, None]
    second_axis = along_second[None, None, :] + shifted[:, 1, None, None]
    return (first_axis * first_axis + second_axis * second_axis <= radius_sq).astype(jnp.float32)


def on_device(mask_field, target_print, source_points, source_groups, group_logits, pupil_radius):
    row_count = mask_field.shape[0]
    length = mask_field.shape[1]
    half_band = K // 2
    device = lax.axis_index("slab")
    positions = device * row_count + jnp.arange(row_count, dtype=jnp.int32)
    everywhere = jnp.arange(length, dtype=jnp.int32)
    frequency = jnp.arange(K, dtype=jnp.int32) - half_band
    cos_full, sin_full = turn_table(everywhere, frequency, length)
    cos_local, sin_local = turn_table(positions, frequency, length)
    cutoff = pupil_radius[0]
    radius_sq = cutoff * cutoff
    shifted = (source_points - GRID // 2) * cutoff // shift_scale
    norming = 1.0 / (length * length)
    row_real = jnp.dot(mask_field, cos_full, precision=highest)
    row_imag = -jnp.dot(mask_field, sin_full, precision=highest)
    spec_real = contract("xk,xj->kj", cos_local, row_real) + contract(
        "xk,xj->kj", sin_local, row_imag
    )
    spec_imag = contract("xk,xj->kj", cos_local, row_imag) - contract(
        "xk,xj->kj", sin_local, row_real
    )
    whole_band = lax.psum(jnp.stack([spec_real, spec_imag], 0), "slab")
    width_here = whole_band.shape[2]
    columns = jnp.arange(width_here, dtype=jnp.int32) - half_band
    passed = pupil_mask(shifted, radius_sq, frequency, columns)
    real_part = passed * whole_band[0][None]
    imag_part = passed * whole_band[1][None]
    lifted_real = contract("xk,skj->sxj", cos_local, real_part) - contract(
        "xk,skj->sxj", sin_local, imag_part
    )
    lifted_imag = contract("xk,skj->sxj", cos_local, imag_part) + contract(
        "xk,skj->sxj", sin_local, real_part
    )
    lifted = jnp.stack([lifted_real, lifted_imag], 1)
    field_real = (
        contract("sxk,yk->sxy", lifted[:, 0], cos_full)
        - contract("sxk,yk->sxy", lifted[:, 1], sin_full)
    ) * norming
    field_imag = (
        contract("sxk,yk->sxy", lifted[:, 0], sin_full)
        + contract("sxk,yk->sxy", lifted[:, 1], cos_full)
    ) * norming
    bright = field_real * field_real + field_imag * field_imag
    onehot_table = (source_groups[:, None] == jnp.arange(NG, dtype=jnp.int32)[None, :]).astype(
        jnp.float32
    )
    weights = jnp.exp(jnp.sum(onehot_table * group_logits[None, :], 1))
    total_weight = jnp.sum(weights)
    weight_share = weights / total_weight
    intensity = jnp.einsum("s,sxy->xy", weight_share, bright, precision=highest)
    resist = jax.nn.sigmoid(steepness * (intensity - threshold))
    misfit = resist - target_print.astype(jnp.float32)
    slope_map = 2.0 * misfit * steepness * resist * (1.0 - resist)
    per_source = contract("sxy,xy->s", bright, slope_map)
    against = jnp.sum(slope_map * intensity)
    squares = jnp.sum(misfit * misfit)
    per_source, against, squares = lax.psum((per_source, against, squares), "slab")
    loss_value = (squares * norming).reshape(1)
    source_pull = weights * (per_source - against) / total_weight
    group_grad = jnp.sum(onehot_table * source_pull[:, None], 0) * norming
    factor = 2.0 * weight_share[:, None, None] * slope_map[None] * norming
    back_real = factor * field_real
    back_imag = factor * field_imag
    down_real = contract("sxy,yk->sxk", back_real, cos_full) + contract(
        "sxy,yk->sxk", back_imag, sin_full
    )
    down_imag = contract("sxy,yk->sxk", back_imag, cos_full) - contract(
        "sxy,yk->sxk", back_real, sin_full
    )
    settle_real = contract("xk,sxj->skj", cos_local, down_real) + contract(
        "xk,sxj->skj", sin_local, down_imag
    )
    settle_imag = contract("xk,sxj->skj", cos_local, down_imag) - contract(
        "xk,sxj->skj", sin_local, down_real
    )
    passed = pupil_mask(shifted, radius_sq, frequency, frequency)
    pull_band = jnp.stack([jnp.sum(passed * settle_real, 0), jnp.sum(passed * settle_imag, 0)], 0)
    whole_pull = lax.psum(pull_band, "slab")
    spread_real = contract("xk,kj->xj", cos_local, whole_pull[0]) - contract(
        "xk,kj->xj", sin_local, whole_pull[1]
    )
    spread_imag = contract("xk,kj->xj", cos_local, whole_pull[1]) + contract(
        "xk,kj->xj", sin_local, whole_pull[0]
    )
    spread_out = jnp.stack([spread_real, spread_imag], 0)
    mask_grad = contract("xk,yk->xy", spread_out[0], cos_full) - contract(
        "xk,yk->xy", spread_out[1], sin_full
    )
    return (loss_value, mask_grad, group_grad)


def solution(mesh):
    in_specs = (
        P(("clip", "slab"), None),
        P(("clip", "slab"), None),
        P("clip", None),
        P("clip"),
        P("clip"),
        P("clip"),
    )
    out_specs = (P("clip"), P(("clip", "slab"), None), P("clip"))
    return jax.shard_map(
        on_device, mesh=mesh, in_specs=in_specs, out_specs=out_specs, check_vma=False
    )
```

profile of v0, /device:TPU:0, one launch (start us, length us, event | category | flops | bytes accessed | tf_op | source)
XLA Modules:
  0.0 627.9 jit_solution(16755961232208500277)
XLA Ops:
  8.4 10.9 %convolution_negate_fusion = f32[256,128]{1,0:T(8,128)S(1)} fusion(f32[128,2048]{1,0:T(8,128)S(1)} %copy-done, s32[256]{0:T(256)S(1)} %iota_add_fusion), kind=kOutput, calls=%fused_computation.93 | convolution fusion | flops 812679168 | bytes 1180672 | tf_op jit(solution)/shard_map/dot_general | solution.py:48
  19.4 11.1 %fusion.112 = f32[256,128]{1,0:T(8,128)S(1)} fusion(f32[128,2048]{1,0:T(8,128)S(1)} %copy-done, s32[256]{0:T(256)S(1)} %iota_add_fusion), kind=kOutput, calls=%fused_computation.110 | convolution fusion | flops 812646400 | bytes 1180672 | tf_op jit(solution)/shard_map/dot_general | solution.py:47
  36.9 92.1 %all-reduce.4.cloned.1.call-done = f32[2,256,256]{2,1,0:T(8,128)} async-done(((f32[2,256,256]{2,1,0:T(8,128)}), f32[2,256,256]{2,1,0:T(8,128)}) %all-reduce.4.cloned.1.call-update) | async-done | bytes 524304 | tf_op jit(solution)/shard_map/psum | solution.py:55
  134.2 5.4 fusion.28
  139.7 6.1 fusion.76
  145.8 37.3 %fusion.41 = f32[16,128,2048]{2,1,0:T(8,128)} fusion(f32[16,256,128]{2,1,0:T(8,128)S(1)} %fusion.76, s32[256]{0:T(256)S(1)} %iota_add_fusion), kind=kOutput, calls=%fused_computation.48 | convolution fusion | flops 12892241920 | bytes 18875392 | tf_op jit(solution)/shard_map/sxk,yk->sxy/dot_general | solution.py:18
  183.2 36.5 %fusion.49 = f32[16,128,2048]{2,1,0:T(8,128)S(1)} fusion(f32[16,256,128]{2,1,0:T(8,128)S(1)} %fusion.76, s32[256]{0:T(256)S(1)} %iota_add_fusion), kind=kOutput, calls=%fused_computation.56 | convolution fusion | flops 12892241920 | bytes 18875392 | tf_op jit(solution)/shard_map/sxk,yk->sxy/dot_general | solution.py:18
  219.7 4.1 fusion.79
  225.2 38.2 %subtract_multiply_fusion = f32[16,128,2048]{2,1,0:T(8,128)} fusion(f32[16,128,2048]{2,1,0:T(8,128)S(1)} %fusion.49, f32[16,256,128]{2,1,0:T(8,128)S(1)} %fusion.79, s32[256]{0:T(256)S(1)} %iota_add_fusion), kind=kOutput, calls=%fused_computation.5 | convolution fusion | flops 12900630528 | bytes 35652608 | tf_op jit(solution)/shard_map/sxk,yk->sxy/dot_general | solution.py:18
  263.4 43.0 %multiply_add_fusion = (f32[16,128,2048]{2,1,0:T(8,128)S(1)}, f32[16,128,2048]{2,1,0:T(8,128)}) fusion(f32[16,128,2048]{2,1,0:T(8,128)} %subtract_multiply_fusion, f32[16,128,2048]{2,1,0:T(8,128)} %fusion.41, s32[256]{0:T(256)S(1)} %iota_add_fusion, f32[16,256,128]{2,1,0:T(8,128)} %copy-done.2), kind=kOutput, calls=%fused_computation.3 | convolution fusion | flops 12913213440 | bytes 69207040 | tf_op jit(solution)/shard_map/sxk,yk->sxy/dot_general | solution.py:18
  306.4 17.7 %fusion.4 = f32[1,128,2048]{2,0,1:T(1,128)S(1)} fusion(f32[16,128,2048]{2,1,0:T(8,128)S(1)} %get-tuple-element.17, f32[]{:T(128)} %exponential_reduce_fusion, f32[16]{0:T(128)S(1)} %select_reduce_fusion.1), kind=kOutput, calls=%fused_computation.8 | convolution fusion | flops 50331664 | bytes 17825860 | tf_op jit(solution)/shard_map/s,sxy->xy/dot_general | solution.py:83
  325.6 25.5 %fusion.94 = f32[16]{0:T(128)} fusion(f32[16,128,2048]{2,1,0:T(8,128)S(1)} %get-tuple-element.17, f32[128,2048,1]{1,0,2:T(8,128)S(1)} %bitcast.127), kind=kOutput, calls=%fused_computation.94 | convolution fusion | flops 50331648 | bytes 17825856 | tf_op jit(solution)/shard_map/sxy,xy->s/dot_general | solution.py:18
  351.1 32.7 %all-reduce = (f32[]{:T(128)}, f32[16]{0:T(128)S(1)}, f32[]{:T(128)}) all-reduce(f32[]{:T(128)} %get-tuple-element.4, f32[16]{0:T(128)} %fusion.94, f32[]{:T(128)} %get-tuple-element.3), channel_id=1, replica_groups=mesh['clip'=2,'slab'=16] {'slab'}, use_global_device_ids=true, to_apply=%region_4.5 | all-reduce | flops 18 | bytes 144 | tf_op jit(solution)/shard_map/psum | solution.py:90
  385.1 25.5 %fusion.6 = f32[16,128,256]{2,1,0:T(8,128)S(1)} fusion(f32[16,128,2048]{2,1,0:T(8,128)} %subtract_multiply_fusion, f32[128,2048]{1,0:T(8,128)S(1)} %get-tuple-element.8, f32[16]{0:T(128)S(1)} %get-tuple-element.16, s32[256]{0:T(256)S(1)} %iota_add_fusion), kind=kOutput, calls=%fused_computation.10 | convolution fusion | flops 12904824832 | bytes 19924032 | tf_op jit(solution)/shard_map/sxy,yk->sxk/dot_general | solution.py:18
  410.6 24.6 %fusion.8 = f32[16,128,256]{2,1,0:T(8,128)S(1)} fusion(f32[16,128,2048]{2,1,0:T(8,128)} %subtract_multiply_fusion, f32[128,2048]{1,0:T(8,128)S(1)} %get-tuple-element.8, f32[16]{0:T(128)S(1)} %get-tuple-element.16, s32[256]{0:T(256)S(1)} %iota_add_fusion), kind=kOutput, calls=%fused_computation.11 | convolution fusion | flops 12904824832 | bytes 19924032 | tf_op jit(solution)/shard_map/sxy,yk->sxk/dot_general | solution.py:18
  435.2 24.9 %fusion.82 = f32[16,128,256]{2,1,0:T(8,128)S(1)} fusion(f32[16,128,256]{2,1,0:T(8,128)S(1)} %fusion.8, f32[16,128,2048]{2,1,0:T(8,128)} %get-tuple-element.18, f32[128,2048]{1,0:T(8,128)S(1)} %get-tuple-element.8, f32[16]{0:T(128)S(1)} %get-tuple-element.16, s32[256]{0:T(256)S(1)} %iota_add_fusion), kind=kOutput, calls=%fused_computation.85 | convolution fusion | flops 12905349120 | bytes 22021184 | tf_op jit(solution)/shard_map/sxy,yk->sxk/dot_general | solution.py:18
  460.1 25.3 %fusion.87 = f32[16,128,256]{2,1,0:T(8,128)S(1)} fusion(f32[16,128,256]{2,1,0:T(8,128)S(1)} %fusion.6, f32[16,128,2048]{2,1,0:T(8,128)} %get-tuple-element.18, f32[128,2048]{1,0:T(8,128)S(1)} %get-tuple-element.8, f32[16]{0:T(128)S(1)} %get-tuple-element.16, s32[256]{0:T(256)S(1)} %iota_add_fusion), kind=kOutput, calls=%fused_computation.86 | convolution fusion | flops 12905349120 | bytes 22021184 | tf_op jit(solution)/shard_map/sxy,yk->sxk/dot_general | solution.py:18
  485.5 4.2 fusion.129
  489.6 4.2 fusion.131
  493.8 5.2 fusion.34
  499.1 5.1 fusion.35
  506.3 86.8 %all-reduce.6.cloned.1.call-done = f32[2,256,256]{1,2,0:T(8,128)} async-done(((f32[2,256,256]{1,2,0:T(8,128)}), f32[2,256,256]{1,2,0:T(8,128)}) %all-reduce.6.cloned.1.call-update) | async-done | bytes 524304 | tf_op jit(solution)/shard_map/psum | solution.py:111
  596.8 9.6 %fusion.109 = f32[128,2048]{1,0:T(8,128)S(1)} fusion(f32[128,256]{1,0:T(8,128)S(1)} %convolution_subtract_fusion.2, s32[256]{0:T(256)S(1)} %iota_add_fusion), kind=kOutput, calls=%fused_computation.109 | convolution fusion | flops 812646400 | bytes 1180672 | tf_op jit(solution)/shard_map/xk,yk->xy/dot_general | solution.py:18
  608.2 11.5 %convolution_subtract_fusion = f32[128,2048]{1,0:T(8,128)} fusion(f32[128,2048]{1,0:T(8,128)S(1)} %fusion.109, f32[128,256]{1,0:T(8,128)S(1)} %convolution_add_fusion.1, s32[256]{0:T(256)S(1)} %iota_add_fusion), kind=kOutput, calls=%fused_computation.42 | convolution fusion | flops 812908544 | bytes 2229248 | tf_op jit(solution)/shard_map/xk,yk->xy/dot_general | solution.py:18
  (55 shorter events, 23.2 us)
Async XLA Ops:
  7.2 1.2 copy-start
  7.2 121.8 %all-reduce.4.cloned.1.call-start = ((), (), s32[]{:S(2)}) async-start(), calls=%async_computation | async-start | bytes 1048576 | tf_op jit(solution)/shard_map/psum | solution.py:55
  30.4 5.6 copy-start.8
  30.4 5.7 copy-start.10
  30.4 5.7 copy-start.11
  35.3 557.8 %all-reduce.6.cloned.1.call-start = ((), (), s32[]{:S(2)}) async-start(), calls=%async_computation.1 | async-start | bytes 1048576 | tf_op jit(solution)/shard_map/psum | solution.py:111
  36.9 182.8 %copy-start.4 = (s32[16,256]{1,0:T(8,128)}, s32[16,256]{1,0:T(8,128)S(1)}, u32[]{:S(2)}) copy-start(s32[16,256]{1,0:T(8,128)S(1)} %get-tuple-element.11) | copy-start | bytes 49156
  36.9 182.8 %copy-start.6 = (s32[16,256]{1,0:T(8,128)}, s32[16,256]{1,0:T(8,128)S(1)}, u32[]{:S(2)}) copy-start(s32[16,256]{1,0:T(8,128)S(1)} %get-tuple-element.12) | copy-start | bytes 49156
  223.9 1.3 copy-start.2
  306.4 17.7 %copy-start.3 = (s32[128,2048]{1,0:T(8,128)S(1)}, s32[128,2048]{1,0:T(8,128)}, u32[]{:S(2)}) copy-start(s32[128,2048]{1,0:T(8,128)} %param.7) | copy-start | bytes 3145732
  489.6 4.2 copy-start.5
  489.6 4.2 copy-start.7
  499.1 5.9 copy-start.12
  596.8 9.6 %copy-start.9 = (f32[2,256,256]{1,2,0:T(8,128)S(1)}, f32[2,256,256]{1,2,0:T(8,128)}, u32[]{:S(2)}) copy-start(f32[2,256,256]{1,2,0:T(8,128)} %all-reduce.6.cloned.1.call-done) | copy-start | bytes 1572868
  608.2 11.5 %copy-start.1 = (f32[128,2048]{1,0:T(8,128)S(1)}, f32[128,2048]{1,0:T(8,128)}, u32[]{:S(2)}) copy-start(f32[128,2048]{1,0:T(8,128)} %param.6) | copy-start | bytes 3145732
Sparse Core Ops, SparseCore 0:
  35.5 93.4 all-reduce.3
  505.1 88.0 all-reduce.5
where the time goes:
time: 637 us; the launch traced here: 628 us
  matrix products  389 us (61%)
  waiting for transfers between devices  179 us (28%)
  blocking collectives  32.7 us (5%)
  between operations  17.1 us (3%)
    dot_general x27, matrix products, contract(): return jnp.einsum(form, left, right, precision=highest)  350 us
    psum x1, waiting for transfers between devices, on_device(): whole_band = lax.psum(jnp.stack([spec_real, spec_imag], 0), 'slab')  92.1 us
    psum x1, waiting for transfers between devices, on_device(): whole_pull = lax.psum(pull_band, 'slab')  86.8 us
    psum x1, blocking collectives, on_device(): lax.psum((per_source, against, squares), 'slab')  32.7 us
    dot_general x1, matrix products, on_device(): intensity = jnp.einsum('s,sxy->xy', weight_share, bright, precision=highest)  17.7 us
  transfers between devices with their start and end apart: 2, of which 2 were waited for; matrix products, arithmetic and copies ran while one was open for 0% of the time, Pallas kernels for 0%

commit v1 on v0

--- a/solution.py
+++ b/solution.py
@@ -108,7 +108,10 @@
     )
     passed = pupil_mask(shifted, radius_sq, frequency, frequency)
     pull_band = jnp.stack([jnp.sum(passed * settle_real, 0), jnp.sum(passed * settle_imag, 0)], 0)
-    whole_pull = lax.psum(pull_band, "slab")
+    size, whole_pull = (lax.axis_size("slab"), pull_band)
+    for far in [1 << k for k in range(size.bit_length() - 1)]:
+        route = [(i, i ^ far) for i in range(size)]
+        whole_pull = whole_pull + lax.ppermute(whole_pull, "slab", route)
     spread_real = contract("xk,kj->xj", cos_local, whole_pull[0]) - contract(
         "xk,kj->xj", sin_local, whole_pull[1]
     )

time: 637 us -> 600 us (0.942)
  waiting for transfers between devices: 179 us -> 144 us
    psum x1 -> x0, waiting for transfers between devices: 86.8 us -> none  [on_device(): whole_pull = lax.psum(pull_band, 'slab')]
    ppermute x0 -> x4, waiting for transfers between devices: none -> 52 us  [on_device(): whole_pull = whole_pull + lax.ppermute(whole_pull, 'slab', route)]
  transfers between devices with their start and end apart: 2 -> 5, of which waited for: 2 -> 5; matrix products, arithmetic and copies ran while one was open for 0% -> 0% of each run, Pallas kernels for 0% -> 0%
where the time goes in v1:
time: 600 us; the launch traced here: 591 us
  matrix products  387 us (64%)
  waiting for transfers between devices  144 us (24%)
  blocking collectives  32.6 us (5%)
  between operations  17.1 us (3%)
    dot_general x27, matrix products, contract(): return jnp.einsum(form, left, right, precision=highest)  348 us
    psum x1, waiting for transfers between devices, on_device(): whole_band = lax.psum(jnp.stack([spec_real, spec_imag], 0), 'slab')  92.2 us
    ppermute x4, waiting for transfers between devices, on_device(): whole_pull = whole_pull + lax.ppermute(whole_pull, 'slab', route)  52 us
    psum x1, blocking collectives, on_device(): lax.psum((per_source, against, squares), 'slab')  32.6 us
    dot_general x1, matrix products, on_device(): intensity = jnp.einsum('s,sxy->xy', weight_share, bright, precision=highest)  17.7 us
  transfers between devices with their start and end apart: 5, of which 5 were waited for; matrix products, arithmetic and copies ran while one was open for 0% of the time, Pallas kernels for 0%

profile of v1, /device:TPU:0, one launch (start us, length us, event | category | flops | bytes accessed | tf_op | source)
XLA Modules:
  0.0 591.0 jit_solution(12933313884918631757)
XLA Ops:
  8.4 10.9 %convolution_negate_fusion = f32[256,128]{1,0:T(8,128)S(1)} fusion(f32[128,2048]{1,0:T(8,128)S(1)} %copy-done, s32[256]{0:T(256)S(1)} %iota_add_fusion), kind=kOutput, calls=%fused_computation.93 | convolution fusion | flops 812679168 | bytes 1180672 | tf_op jit(solution)/shard_map/dot_general | solution.py:48
  19.4 11.1 %fusion.112 = f32[256,128]{1,0:T(8,128)S(1)} fusion(f32[128,2048]{1,0:T(8,128)S(1)} %copy-done, s32[256]{0:T(256)S(1)} %iota_add_fusion), kind=kOutput, calls=%fused_computation.110 | convolution fusion | flops 812646400 | bytes 1180672 | tf_op jit(solution)/shard_map/dot_general | solution.py:47
  36.8 92.2 %all-reduce.3.cloned.1.call-done = f32[2,256,256]{2,1,0:T(8,128)} async-done(((f32[2,256,256]{2,1,0:T(8,128)}), f32[2,256,256]{2,1,0:T(8,128)}) %all-reduce.3.cloned.1.call-update) | async-done | bytes 524304 | tf_op jit(solution)/shard_map/psum | solution.py:55
  134.2 5.4 fusion.28
  139.7 6.1 %fusion.76 = f32[16,256,128]{2,1,0:T(8,128)S(1)} fusion(f32[16,256,128]{2,1,0:T(8,128)} %fusion.28, f32[256,256]{0,1:T(8,128)S(1)} %copy.29, s32[]{:T(128)S(6)} %mul.247, s32[16,256]{1,0:T(8,128)S(1)} %get-tuple-element.12, s32[16,256]{1,0:T(8,128)S(1)} %get-tuple-element.11, s32[256]{0:T(256)S(1)} %iota_add_fusion, s32[128]{0:T(128)S(1)} %iota_add_fusion.1), kind=kOutput, calls=%fused_computation.83 | convolution fusion | flops 1614741504 | bytes 4490756 | tf_op jit(solution)/shard_map/xk,skj->sxj/dot_general | solution.py:18
  145.8 37.3 %fusion.41 = f32[16,128,2048]{2,1,0:T(8,128)} fusion(f32[16,256,128]{2,1,0:T(8,128)S(1)} %fusion.76, s32[256]{0:T(256)S(1)} %iota_add_fusion), kind=kOutput, calls=%fused_computation.48 | convolution fusion | flops 12892241920 | bytes 18875392 | tf_op jit(solution)/shard_map/sxk,yk->sxy/dot_general | solution.py:18
  183.2 36.5 %fusion.49 = f32[16,128,2048]{2,1,0:T(8,128)S(1)} fusion(f32[16,256,128]{2,1,0:T(8,128)S(1)} %fusion.76, s32[256]{0:T(256)S(1)} %iota_add_fusion), kind=kOutput, calls=%fused_computation.56 | convolution fusion | flops 12892241920 | bytes 18875392 | tf_op jit(solution)/shard_map/sxk,yk->sxy/dot_general | solution.py:18
  225.2 38.2 %subtract_multiply_fusion = f32[16,128,2048]{2,1,0:T(8,128)} fusion(f32[16,128,2048]{2,1,0:T(8,128)S(1)} %fusion.49, f32[16,256,128]{2,1,0:T(8,128)S(1)} %fusion.79, s32[256]{0:T(256)S(1)} %iota_add_fusion), kind=kOutput, calls=%fused_computation.5 | convolution fusion | flops 12900630528 | bytes 35652608 | tf_op jit(solution)/shard_map/sxk,yk->sxy/dot_general | solution.py:18
  263.4 43.0 %multiply_add_fusion = (f32[16,128,2048]{2,1,0:T(8,128)S(1)}, f32[16,128,2048]{2,1,0:T(8,128)}) fusion(f32[16,128,2048]{2,1,0:T(8,128)} %subtract_multiply_fusion, f32[16,128,2048]{2,1,0:T(8,128)} %fusion.41, s32[256]{0:T(256)S(1)} %iota_add_fusion, f32[16,256,128]{2,1,0:T(8,128)} %copy-done.2), kind=kOutput, calls=%fused_computation.3 | convolution fusion | flops 12913213440 | bytes 69207040 | tf_op jit(solution)/shard_map/sxk,yk->sxy/dot_general | solution.py:18
  306.4 17.7 %fusion.4 = f32[1,128,2048]{2,0,1:T(1,128)S(1)} fusion(f32[16,128,2048]{2,1,0:T(8,128)S(1)} %get-tuple-element.17, f32[]{:T(128)} %exponential_reduce_fusion, f32[16]{0:T(128)S(1)} %select_reduce_fusion.1), kind=kOutput, calls=%fused_computation.8 | convolution fusion | flops 50331664 | bytes 17825860 | tf_op jit(solution)/shard_map/s,sxy->xy/dot_general | solution.py:83
  325.6 25.5 %fusion.94 = f32[16]{0:T(128)} fusion(f32[16,128,2048]{2,1,0:T(8,128)S(1)} %get-tuple-element.17, f32[128,2048,1]{1,0,2:T(8,128)S(1)} %bitcast.127), kind=kOutput, calls=%fused_computation.94 | convolution fusion | flops 50331648 | bytes 17825856 | tf_op jit(solution)/shard_map/sxy,xy->s/dot_general | solution.py:18
  351.1 32.6 %all-reduce = (f32[]{:T(128)}, f32[16]{0:T(128)S(1)}, f32[]{:T(128)}) all-reduce(f32[]{:T(128)} %get-tuple-element.4, f32[16]{0:T(128)} %fusion.94, f32[]{:T(128)} %get-tuple-element.3), channel_id=1, replica_groups=mesh['clip'=2,'slab'=16] {'slab'}, use_global_device_ids=true, to_apply=%region_4.5 | all-reduce | flops 18 | bytes 144 | tf_op jit(solution)/shard_map/psum | solution.py:90
  385.1 25.5 %fusion.6 = f32[16,128,256]{2,1,0:T(8,128)S(1)} fusion(f32[16,128,2048]{2,1,0:T(8,128)} %subtract_multiply_fusion, f32[128,2048]{1,0:T(8,128)S(1)} %get-tuple-element.8, f32[16]{0:T(128)S(1)} %get-tuple-element.16, s32[256]{0:T(256)S(1)} %iota_add_fusion), kind=kOutput, calls=%fused_computation.10 | convolution fusion | flops 12904824832 | bytes 19924032 | tf_op jit(solution)/shard_map/sxy,yk->sxk/dot_general | solution.py:18
  410.5 24.6 %fusion.8 = f32[16,128,256]{2,1,0:T(8,128)S(1)} fusion(f32[16,128,2048]{2,1,0:T(8,128)} %subtract_multiply_fusion, f32[128,2048]{1,0:T(8,128)S(1)} %get-tuple-element.8, f32[16]{0:T(128)S(1)} %get-tuple-element.16, s32[256]{0:T(256)S(1)} %iota_add_fusion), kind=kOutput, calls=%fused_computation.11 | convolution fusion | flops 12904824832 | bytes 19924032 | tf_op jit(solution)/shard_map/sxy,yk->sxk/dot_general | solution.py:18
  435.2 24.9 %fusion.82 = f32[16,128,256]{2,1,0:T(8,128)S(1)} fusion(f32[16,128,256]{2,1,0:T(8,128)S(1)} %fusion.8, f32[16,128,2048]{2,1,0:T(8,128)} %get-tuple-element.18, f32[128,2048]{1,0:T(8,128)S(1)} %get-tuple-element.8, f32[16]{0:T(128)S(1)} %get-tuple-element.16, s32[256]{0:T(256)S(1)} %iota_add_fusion), kind=kOutput, calls=%fused_computation.85 | convolution fusion | flops 12905349120 | bytes 22021184 | tf_op jit(solution)/shard_map/sxy,yk->sxk/dot_general | solution.py:18
  460.1 25.3 %fusion.87 = f32[16,128,256]{2,1,0:T(8,128)S(1)} fusion(f32[16,128,256]{2,1,0:T(8,128)S(1)} %fusion.6, f32[16,128,2048]{2,1,0:T(8,128)} %get-tuple-element.18, f32[128,2048]{1,0:T(8,128)S(1)} %get-tuple-element.8, f32[16]{0:T(128)S(1)} %get-tuple-element.16, s32[256]{0:T(256)S(1)} %iota_add_fusion), kind=kOutput, calls=%fused_computation.86 | convolution fusion | flops 12905349120 | bytes 22021184 | tf_op jit(solution)/shard_map/sxy,yk->sxk/dot_general | solution.py:18
  485.4 4.2 fusion.129
  493.8 5.2 fusion.34
  499.1 5.1 fusion.35
  506.3 14.0 %collective-permute-done.1 = f32[2,256,256]{1,2,0:T(8,128)S(1)} collective-permute-done((f32[2,256,256]{1,2,0:T(8,128)S(1)}, f32[2,256,256]{1,2,0:T(8,128)S(1)}, u32[]{:S(2)}, u32[]{:S(2)}) %collective-permute-start.1) | collective-permute-done | bytes 524320 | tf_op jit(solution)/shard_map/ppermute | solution.py:114
  520.4 13.1 %collective-permute-done.2 = f32[2,256,256]{1,2,0:T(8,128)S(1)} collective-permute-done((f32[2,256,256]{1,2,0:T(8,128)S(1)}, f32[2,256,256]{1,2,0:T(8,128)S(1)}, u32[]{:S(2)}, u32[]{:S(2)}) %collective-permute-start.2) | collective-permute-done | bytes 524320 | tf_op jit(solution)/shard_map/ppermute | solution.py:114
  535.0 23.1 %collective-permute-done.3 = f32[2,256,256]{1,2,0:T(8,128)S(1)} collective-permute-done((f32[2,256,256]{1,2,0:T(8,128)S(1)}, f32[2,256,256]{1,2,0:T(8,128)S(1)}, u32[]{:S(2)}, u32[]{:S(2)}) %collective-permute-start.3) | collective-permute-done | bytes 524320 | tf_op jit(solution)/shard_map/ppermute | solution.py:114
  561.6 9.6 %fusion.109 = f32[128,2048]{1,0:T(8,128)S(1)} fusion(f32[128,256]{1,0:T(8,128)S(1)} %convolution_subtract_fusion.2, s32[256]{0:T(256)S(1)} %iota_add_fusion), kind=kOutput, calls=%fused_computation.109 | convolution fusion | flops 812646400 | bytes 1180672 | tf_op jit(solution)/shard_map/xk,yk->xy/dot_general | solution.py:18
  571.2 11.5 %convolution_subtract_fusion = f32[128,2048]{1,0:T(8,128)} fusion(f32[128,2048]{1,0:T(8,128)S(1)} %fusion.109, f32[128,256]{1,0:T(8,128)S(1)} %convolution_add_fusion.1, s32[256]{0:T(256)S(1)} %iota_add_fusion), kind=kOutput, calls=%fused_computation.42 | convolution fusion | flops 812908544 | bytes 2229248 | tf_op jit(solution)/shard_map/xk,yk->xy/dot_general | solution.py:18
  (62 shorter events, 31.2 us)
Async XLA Ops:
  7.2 1.2 copy-start
  7.2 121.8 %all-reduce.3.cloned.1.call-start = ((), (), s32[]{:S(2)}) async-start(), calls=%async_computation | async-start | bytes 1048576 | tf_op jit(solution)/shard_map/psum | solution.py:55
  30.4 5.6 copy-start.8
  30.4 5.6 copy-start.9
  30.4 5.6 copy-start.10
  36.8 182.9 %copy-start.4 = (s32[16,256]{1,0:T(8,128)}, s32[16,256]{1,0:T(8,128)S(1)}, u32[]{:S(2)}) copy-start(s32[16,256]{1,0:T(8,128)S(1)} %get-tuple-element.11) | copy-start | bytes 49156
  36.8 182.9 %copy-start.6 = (s32[16,256]{1,0:T(8,128)}, s32[16,256]{1,0:T(8,128)S(1)}, u32[]{:S(2)}) copy-start(s32[16,256]{1,0:T(8,128)S(1)} %get-tuple-element.12) | copy-start | bytes 49156
  223.9 1.3 copy-start.2
  306.4 17.7 %copy-start.3 = (s32[128,2048]{1,0:T(8,128)S(1)}, s32[128,2048]{1,0:T(8,128)}, u32[]{:S(2)}) copy-start(s32[128,2048]{1,0:T(8,128)} %param.7) | copy-start | bytes 3145732
  489.6 4.2 copy-start.5
  489.6 4.2 copy-start.7
  504.2 2.0 collective-permute-start
  506.2 28.1 %copy-start.11 = (s32[16]{0:T(128)S(1)}, s32[16]{0:T(128)}, u32[]{:S(2)}) copy-start(s32[16]{0:T(128)} %param.9) | copy-start | bytes 196
  506.2 14.0 %collective-permute-start.1 = (f32[2,256,256]{1,2,0:T(8,128)S(1)}, f32[2,256,256]{1,2,0:T(8,128)S(1)}, u32[]{:S(2)}, u32[]{:S(2)}) collective-permute-start(f32[2,256,256]{1,2,0:T(8,128)S(1)} %fusion.276), channel_id=1, source_target_pairs={{0,2},{1,3},{2,0},{3,1},{4,6},{5,7},{6,4},{7,5},{8,10},{9,11},{10,... | collective-permute-start | bytes 1572872 | tf_op jit(solution)/shard_map/ppermute | solution.py:114
  520.4 13.2 %collective-permute-start.2 = (f32[2,256,256]{1,2,0:T(8,128)S(1)}, f32[2,256,256]{1,2,0:T(8,128)S(1)}, u32[]{:S(2)}, u32[]{:S(2)}) collective-permute-start(f32[2,256,256]{1,2,0:T(8,128)S(1)} %fusion.289), channel_id=1, source_target_pairs={{0,4},{1,5},{2,6},{3,7},{4,0},{5,1},{6,2},{7,3},{8,12},{9,13},{10,... | collective-permute-start | bytes 1572872 | tf_op jit(solution)/shard_map/ppermute | solution.py:114
  533.6 24.5 %collective-permute-start.3 = (f32[2,256,256]{1,2,0:T(8,128)S(1)}, f32[2,256,256]{1,2,0:T(8,128)S(1)}, u32[]{:S(2)}, u32[]{:S(2)}) collective-permute-start(f32[2,256,256]{1,2,0:T(8,128)S(1)} %add.206), channel_id=1, source_target_pairs={{0,8},{1,9},{2,10},{3,11},{4,12},{5,13},{6,14},{7,15},{8,0},{9,1},... | collective-permute-start | bytes 1572872 | tf_op jit(solution)/shard_map/ppermute | solution.py:114
  571.2 11.5 %copy-start.1 = (f32[128,2048]{1,0:T(8,128)S(1)}, f32[128,2048]{1,0:T(8,128)}, u32[]{:S(2)}) copy-start(f32[128,2048]{1,0:T(8,128)} %param.6) | copy-start | bytes 3145732
Sparse Core Ops, SparseCore 0:
  35.5 93.4 all-reduce.2
